TPU v7x, 256 devices: a whole 4x4x8 slice. The times are simulated.
256 devices in a mesh: row: 32 (over z, y_lo, core), col: 8 (over x, y_hi).
Axes of the slice: x: 4, y: 4 (y_hi: 2, y_lo: 2; y = y_hi * 2 + y_lo), z: 8, core: 2. Of those that a mesh axis runs over, the one named last changes fastest.
Arguments:
- acts: bfloat16 [1024, 16384], P(None, 'col'), may hold values from -6 to 6
- grads: bfloat16 [1024, 16384], P(None, 'row'), may hold values from -0.1875 to 0.1875
- row_roots: bfloat16 [16384, 1024], P('row'), as said below
- col_stats: float32 [1024, 16384], P('row', 'col'), as said below
Outputs:
- update: bfloat16 [16384, 16384], P('row', 'col')
- new_stats: float32 [1024, 16384], P('row', 'col')
- new_roots: float32 [1024, 16384], P('row', 'col')
Inputs may be any that keep to these rules, and one draw needn't show every extreme that they name: `col_stats`: each block of 1024 columns is symmetric positive definite. `row_roots`: each block of 1024 rows is symmetric.
All inputs are finite; a program needn't handle non-finite values.
Results may differ from a plain program's by a relative error of at most 0.0015.
The roundings to bfloat16 on the way count: a program that leaves them out, or rounds other values in their place, can miss the bound.
Values may be sent and summed in bfloat16 or wider, within the bound.
No kernel may reach another device: no remote copies, remote signals or barrier semaphores. Data moves between devices by JAX's collectives and lax.ppermute only.
A program may use at most 128 MiB of HBM per device.

v0:
```python
import jax
import jax.numpy as jnp
from jax import lax
from jax.sharding import PartitionSpec as P

decay_rate = 0.75
damping = 0.001
epsilon = 1e-06


def partner(block, axis, bit):
    count = lax.axis_size(axis)
    route = []
    for low in range(count):
        high = low | 1 << bit
        if high != low and high < count:
            route += [(low, high), (high, low)]
    return lax.ppermute(block, axis, route)


def shards(acts, grads, row_roots, col_stats):
    contract_first = (((0,), (0,)), ((), ()))
    block_size = row_roots.shape[1]
    weight_rows = grads.shape[1]
    weight_cols = acts.shape[1]
    stat_rows = col_stats.shape[0]
    block_count = weight_cols // block_size
    total_rows = weight_rows * lax.axis_size("row")
    own_tile = lax.dot_general(
        grads, acts, contract_first, preferred_element_type=jnp.float32
    ).astype(jnp.bfloat16)
    other_tile = partner(own_tile, "row", 0)
    is_lower = lax.axis_index("row") % 2 == 0
    paired = jnp.where(
        is_lower,
        jnp.concatenate([own_tile, other_tile], 0),
        jnp.concatenate([other_tile, own_tile], 0),
    )
    whitened = jnp.dot(row_roots, paired, preferred_element_type=jnp.float32).astype(jnp.bfloat16)
    pieces = []
    for column_index_block in range(block_count):
        left = lax.dynamic_slice_in_dim(
            whitened, column_index_block * block_size, stat_rows * lax.axis_size("row"), 1
        )
        right = whitened[:, column_index_block * block_size : (column_index_block + 1) * block_size]
        pieces.append(
            lax.dot_general(left, right, contract_first, preferred_element_type=jnp.float32)
        )
    summed = lax.psum_scatter(jnp.concatenate(pieces, 1), "row", scatter_dimension=0, tiled=True)
    mix = (1.0 - decay_rate) / total_rows
    new_stats = decay_rate * col_stats + mix * summed
    full_stats = lax.all_gather(new_stats, "row", axis=0, tiled=True)
    first_row = lax.axis_index("row") * stat_rows
    identity = jnp.eye(block_size, dtype=jnp.float32)
    row_iota = lax.broadcasted_iota(jnp.int32, (stat_rows, block_size), 0) + first_row
    col_iota = lax.broadcasted_iota(jnp.int32, (stat_rows, block_size), 1)
    identity_rows = (row_iota == col_iota).astype(jnp.float32)
    scales = []
    starts = []
    factors = []
    for index_block in range(block_count):
        shifted = (
            full_stats[:, index_block * block_size : (index_block + 1) * block_size]
            + damping * identity
        )
        norm_scale = 2.0 * jnp.trace(shifted) / block_size
        start_iterate = shifted / norm_scale
        scales.append(norm_scale)
        starts.append(start_iterate)
        factors.append(1.5 * identity - 0.5 * start_iterate)
    seconds = [
        jnp.dot(starts[k], factors[k], precision=lax.Precision.HIGHEST) for k in range(block_count)
    ]
    root_pieces = []
    for index_block in range(block_count):
        factor_rows = lax.dynamic_slice_in_dim(factors[index_block], first_row, stat_rows, 0)
        product_rows = jnp.dot(factor_rows, seconds[index_block], precision=lax.Precision.HIGHEST)
        second_factor = 1.5 * identity_rows - 0.5 * product_rows
        root_rows = jnp.dot(second_factor, factors[index_block], precision=lax.Precision.HIGHEST)
        root_pieces.append(root_rows / jnp.sqrt(scales[index_block]))
    new_roots = jnp.concatenate(root_pieces, 1)
    roots_half = new_roots.astype(jnp.bfloat16)
    empty = jnp.zeros((weight_rows, weight_cols), jnp.float32)
    piece = lax.all_gather(roots_half, "row", axis=0, tiled=True)
    terms = []
    for index_block in range(block_count):
        left = lax.dynamic_slice_in_dim(whitened, index_block * block_size, piece.shape[0], 1)
        right = piece[:, index_block * block_size : (index_block + 1) * block_size]
        terms.append(jnp.dot(left, right, preferred_element_type=jnp.float32))
    product = empty + jnp.concatenate(terms, 1)
    grad_square = jnp.sum(jnp.square(own_tile.astype(jnp.float32)))
    prod_square = jnp.sum(jnp.square(product))
    grad_total, prod_total = lax.psum((grad_square, prod_square), ("row", "col"))
    update = (product * jnp.sqrt(grad_total / (prod_total + epsilon))).astype(jnp.bfloat16)
    return (update, new_stats, new_roots)


def solution(mesh):
    return jax.shard_map(
        shards,
        mesh=mesh,
        in_specs=(P(None, "col"), P(None, "row"), P("row", None), P("row", "col")),
        out_specs=(P("row", "col"), P("row", "col"), P("row", "col")),
        check_vma=False,
    )
```

profile of v0, /device:TPU:1, one launch (start us, length us, event | category | flops | bytes accessed | tf_op | source)
XLA Modules:
  0.0 459.7 jit_solution(10663552201860508157)
XLA Ops:
  8.4 5.7 %multiply_reduce_fusion.1 = (f32[]{:T(128)}, bf16[512,2048]{1,0:T(8,128)(2,1)S(1)}) fusion(bf16[1024,512]{1,0:T(8,128)(2,1)S(1)} %copy-done, bf16[1024,2048]{1,0:T(8,128)(2,1)} %param.4), kind=kOutput, calls=%fused_computation.15 | convolution fusion | flops 2151677952 | bytes 7340036 | tf_op jit(solution)/shard_map/dot_general | solution.py:29
  14.1 3.2 collective-permute-start
  17.4 3.9 collective-permute-done
  21.3 4.9 %fusion.10 = bf16[512,2048]{0,1:T(8,128)(2,1)S(1)} fusion(bf16[512,1024]{1,0:T(8,128)(2,1)} %param.6, bf16[512,2048]{1,0:T(8,128)(2,1)} %collective-permute-done, bf16[512,2048]{1,0:T(8,128)(2,1)S(1)} %get-tuple-element.18, pred[]{:T(512)S(6)} %eq.24), kind=kOutput, calls=%fused_computation.24 | convolution fusion | flops 2167406592 | bytes 7340033 | tf_op jit(solution)/shard_map/dot_general | solution.py:39
  27.5 1.3 fusion.21
  28.8 4.1 pad_maximum_fusion
  32.9 9.2 %copy.12 = f32[1024,2048]{1,0:T(8,128)} copy(f32[1024,2048]{0,1:T(8,128)} %pad_maximum_fusion) | data formatting | bytes 16777216
  43.4 126.7 %reduce-scatter.4.cloned.1.call-done = f32[32,2048]{1,0:T(8,128)} async-done(((f32[1024,2048]{1,0:T(8,128)}), f32[32,2048]{1,0:T(8,128)}) %reduce-scatter.4.cloned.1.call-update) | async-done | bytes 262160
  172.6 74.8 %all-gather.3.cloned.1.call-done = f32[1024,2048]{1,0:T(8,128)} async-done(((f32[32,2048]{1,0:T(8,128)}), f32[1024,2048]{1,0:T(8,128)}) %all-gather.3.cloned.1.call-update) | async-done | bytes 8388624 | tf_op jit(solution)/shard_map/all_gather | solution.py:52
  247.3 4.3 select_reduce_fusion.1
  253.1 5.1 %select_subtract_fusion.1 = (f32[1024,1024]{1,0:T(8,128)S(1)}, f32[1024,1024]{1,0:T(8,128)S(1)}) fusion(f32[]{:T(128)S(6)} %div.33, f32[1024,2048]{1,0:T(8,128)} %all-gather.3.cloned.1.call-done, f32[]{:T(128)S(6)} %div.38), kind=kLoop, calls=%fused_computation.4 | loop fusion | flops 11534336 | bytes 16777224 | tf_op jit(solution)/shard_map/sub | solution.py:70
  258.9 13.5 %fusion.25 = f32[1024,1024]{1,0:T(8,128)S(1)} fusion(f32[1024,1024]{1,0:T(8,128)S(1)} %get-tuple-element.15, f32[1024,2048]{1,0:T(8,128)S(1)} %copy-done.2, f32[]{:T(128)S(6)} %div.33), kind=kOutput, calls=%fused_computation.43 | convolution fusion | flops 12889096192 | bytes 12582916 | tf_op jit(solution)/shard_map/dot_general | solution.py:72
  272.4 2.7 fusion.16
  275.0 13.7 %fusion.23 = f32[1024,1024]{1,0:T(8,128)S(1)} fusion(f32[1024,1024]{1,0:T(8,128)S(1)} %get-tuple-element.16, f32[1024,2048]{1,0:T(8,128)S(1)} %copy-done.2, f32[]{:T(128)S(6)} %div.38), kind=kOutput, calls=%fused_computation.42 | convolution fusion | flops 12889096192 | bytes 12582916 | tf_op jit(solution)/shard_map/dot_general | solution.py:72
  288.7 2.5 fusion.15
  291.2 2.5 convolution_divide_fusion.1
  293.7 2.5 convolution_divide_fusion
  297.0 66.9 %all-gather.5.cloned.1.call-done = bf16[1024,2048]{1,0:T(8,128)(2,1)} async-done(((bf16[32,2048]{1,0:T(8,128)(2,1)}), bf16[1024,2048]{1,0:T(8,128)(2,1)}) %all-gather.5.cloned.1.call-update) | async-done | bytes 4194320 | tf_op jit(solution)/shard_map/all_gather | solution.py:84
  363.9 3.3 fusion.13
  367.2 2.5 fusion.11
  369.7 1.3 copy-done.3
  371.1 1.7 multiply_reduce_fusion
  372.7 75.5 %all-reduce = (f32[]{:T(128)}, f32[]{:T(128)}) all-reduce(f32[]{:T(128)} %get-tuple-element.17, f32[]{:T(128)} %multiply_reduce_fusion), channel_id=1, replica_groups=mesh['row'=32,'col'=8] {'row','col'}, use_global_device_ids=true, to_apply=%region_4.5 | all-reduce | flops 2 | bytes 16 | tf_op jit(solution)/shard_map/psum | solution.py:93
  449.5 3.4 multiply_convert_fusion
  (26 shorter events, 7.7 us)
Async XLA Ops:
  7.2 1.2 copy-start
  7.2 162.9 %reduce-scatter.4.cloned.1.call-start = ((), (), s32[]{:S(2)}) async-start(), calls=%async_computation.3 | async-start | bytes 8650752
  14.1 7.2 %collective-permute-start = (bf16[512,2048]{1,0:T(8,128)(2,1)S(1)}, bf16[512,2048]{1,0:T(8,128)(2,1)}, u32[]{:S(2)}, u32[]{:S(2)}) collective-permute-start(bf16[512,2048]{1,0:T(8,128)(2,1)S(1)} %get-tuple-element.18), channel_id=1, source_target_pairs={{0,8},{8,0},{16,24},{24,16},{32,40},{40,32},{48,56},{56,48},{64,72... | collective-permute-start | bytes 6291464 | tf_op jit(solution)/shard_map/ppermute | solution.py:18
  26.2 2.6 copy-start.6
  42.1 0.9 copy-start.4
  42.1 205.2 %all-gather.3.cloned.1.call-start = ((), (), s32[]{:S(2)}) async-start(), calls=%async_computation.1 | async-start | bytes 8650752 | tf_op jit(solution)/shard_map/all_gather | solution.py:52
  172.5 191.4 %all-gather.5.cloned.1.call-start = ((), (), s32[]{:S(2)}) async-start(), calls=%async_computation.2 | async-start | bytes 4325376 | tf_op jit(solution)/shard_map/all_gather | solution.py:84
  253.1 5.8 %copy-start.2 = (f32[1024,2048]{1,0:T(8,128)S(1)}, f32[1024,2048]{1,0:T(8,128)}, u32[]{:S(2)}) copy-start(f32[1024,2048]{1,0:T(8,128)} %all-gather.3.cloned.1.call-done) | copy-start | bytes 25165828
  363.9 3.3 copy-start.5
  369.7 1.3 copy-start.3
  371.1 81.9 %copy-start.1 = (bf16[1024,512]{1,0:T(8,128)(2,1)S(1)}, bf16[1024,512]{1,0:T(8,128)(2,1)}, u32[]{:S(2)}) copy-start(bf16[1024,512]{1,0:T(8,128)(2,1)} %param.5) | copy-start | bytes 3145732
Sparse Core Ops, SparseCore 0:
  42.3 127.7 reduce-scatter.3
  172.6 74.6 all-gather.2
  297.1 66.6 all-gather.4
where the time goes:
time: 468 us; the launch traced here: 460 us
  waiting for transfers between devices  272 us (58%)
  blocking collectives  75.5 us (16%)
  matrix products  56.4 us (12%)
  other arithmetic  19.5 us (4%)
  between operations  16.9 us (4%)
  local copies, waits for them, and re-layouts  15.9 us (3%)
    unnamed x4, waiting for transfers between devices  127 us
    psum x1, blocking collectives, shards(): lax.psum((grad_square, prod_square), ('row', 'col'))  75.5 us
    all_gather x1, waiting for transfers between devices, shards(): full_stats = lax.all_gather(new_stats, 'row', axis=0, tiled=True)  74.8 us
    all_gather x1, waiting for transfers between devices, shards(): piece = lax.all_gather(roots_half, 'row', axis=0, tiled=True)  66.9 us
    dot_general x2, matrix products, shards(): jnp.dot(starts[k], factors[k], precision=lax.Precision.HIGHEST)  27.2 us
    unnamed x17, local copies, waits for them, and re-layouts  14.9 us
  transfers between devices with their start and end apart: 4, of which 4 were waited for; matrix products, arithmetic and copies ran while one was open for 0% of the time, Pallas kernels for 0%

commit v1 on v0

--- a/solution.py
+++ b/solution.py
@@ -81,7 +81,9 @@
     new_roots = jnp.concatenate(root_pieces, 1)
     roots_half = new_roots.astype(jnp.bfloat16)
     empty = jnp.zeros((weight_rows, weight_cols), jnp.float32)
-    piece = lax.all_gather(roots_half, "row", axis=0, tiled=True)
+    piece = jnp.concatenate(
+        lax.all_to_all(jnp.stack([roots_half] * lax.axis_size("row")), "row", 0, 0), axis=0
+    )
     terms = []
     for index_block in range(block_count):
         left = lax.dynamic_slice_in_dim(whitened, index_block * block_size, piece.shape[0], 1)

time: 468 us -> 500 us (1.068)
  blocking collectives: 75.5 us -> 178 us
  waiting for transfers between devices: 272 us -> 205 us
    all_to_all x0 -> x1, blocking collectives: none -> 102 us  [shards(): lax.all_to_all(jnp.stack([roots_half] * lax.axis_size('row')), 'row', 0, 0)]
    all_gather x1 -> x0, waiting for transfers between devices: 66.9 us -> none  [shards(): piece = lax.all_gather(roots_half, 'row', axis=0, tiled=True)]
    unnamed x4 -> x3, waiting for transfers between devices: 127 us -> 127 us
  transfers between devices with their start and end apart: 4 -> 3, of which waited for: 4 -> 3; matrix products, arithmetic and copies ran while one was open for 0% -> 0% of each run, Pallas kernels for 0% -> 0%
where the time goes in v1:
time: 500 us; the launch traced here: 492 us
  waiting for transfers between devices  205 us (41%)
  blocking collectives  178 us (36%)
  matrix products  53.1 us (11%)
  other arithmetic  19.4 us (4%)
  between operations  17.1 us (3%)
  local copies, waits for them, and re-layouts  16.4 us (3%)
    unnamed x3, waiting for transfers between devices  127 us
    all_to_all x1, blocking collectives, shards(): lax.all_to_all(jnp.stack([roots_half] * lax.axis_size('row')), 'row', 0, 0)  102 us
    psum x1, blocking collectives, shards(): lax.psum((grad_square, prod_square), ('row', 'col'))  75.9 us
    all_gather x1, waiting for transfers between devices, shards(): full_stats = lax.all_gather(new_stats, 'row', axis=0, tiled=True)  74.6 us
    dot_general x2, matrix products, shards(): jnp.dot(starts[k], factors[k], precision=lax.Precision.HIGHEST)  27.2 us
    unnamed x17, local copies, waits for them, and re-layouts  14.9 us
  transfers between devices with their start and end apart: 3, of which 3 were waited for; matrix products, arithmetic and copies ran while one was open for 0% of the time, Pallas kernels for 0%

profile of v1, /device:TPU:1, one launch (start us, length us, event | category | flops | bytes accessed | tf_op | source)
XLA Modules:
  0.0 492.2 jit_solution(3377409923242977265)
XLA Ops:
  8.4 5.7 %multiply_reduce_fusion.1 = (f32[]{:T(128)}, bf16[512,2048]{1,0:T(8,128)(2,1)S(1)}) fusion(bf16[1024,512]{1,0:T(8,128)(2,1)S(1)} %copy-done, bf16[1024,2048]{1,0:T(8,128)(2,1)} %param.4), kind=kOutput, calls=%fused_computation.15 | convolution fusion | flops 2151677952 | bytes 7340036 | tf_op jit(solution)/shard_map/dot_general | solution.py:29
  14.1 3.2 collective-permute-start
  17.4 3.9 collective-permute-done
  21.3 4.9 fusion.10
  26.2 1.3 fusion.18
  27.5 1.3 fusion.21
  28.8 4.1 pad_maximum_fusion
  32.9 9.2 %copy.12 = f32[1024,2048]{1,0:T(8,128)} copy(f32[1024,2048]{0,1:T(8,128)} %pad_maximum_fusion) | data formatting | bytes 16777216
  43.3 126.8 %reduce-scatter.4.cloned.1.call-done = f32[32,2048]{1,0:T(8,128)} async-done(((f32[1024,2048]{1,0:T(8,128)}), f32[32,2048]{1,0:T(8,128)}) %reduce-scatter.4.cloned.1.call-update) | async-done | bytes 262160
  170.1 1.3 copy.13
  172.6 74.6 %all-gather.2.cloned.1.call-done = f32[1024,2048]{1,0:T(8,128)} async-done(((f32[32,2048]{1,0:T(8,128)}), f32[1024,2048]{1,0:T(8,128)}) %all-gather.2.cloned.1.call-update) | async-done | bytes 8388624 | tf_op jit(solution)/shard_map/all_gather | solution.py:52
  247.2 4.2 select_reduce_fusion.1
  252.7 5.1 %select_subtract_fusion.1 = (f32[1024,1024]{1,0:T(8,128)S(1)}, f32[1024,1024]{1,0:T(8,128)S(1)}) fusion(f32[]{:T(128)S(6)} %div.33, f32[1024,2048]{1,0:T(8,128)} %all-gather.2.cloned.1.call-done, f32[]{:T(128)S(6)} %div.38), kind=kLoop, calls=%fused_computation.4 | loop fusion | flops 11534336 | bytes 16777224 | tf_op jit(solution)/shard_map/sub | solution.py:70
  258.6 13.5 %fusion.25 = f32[1024,1024]{1,0:T(8,128)S(1)} fusion(f32[1024,1024]{1,0:T(8,128)S(1)} %get-tuple-element.15, f32[1024,2048]{1,0:T(8,128)S(1)} %copy-done.2, f32[]{:T(128)S(6)} %div.33), kind=kOutput, calls=%fused_computation.43 | convolution fusion | flops 12889096192 | bytes 12582916 | tf_op jit(solution)/shard_map/dot_general | solution.py:72
  272.0 2.7 fusion.16
  274.7 13.7 %fusion.23 = f32[1024,1024]{1,0:T(8,128)S(1)} fusion(f32[1024,1024]{1,0:T(8,128)S(1)} %get-tuple-element.16, f32[1024,2048]{1,0:T(8,128)S(1)} %copy-done.2, f32[]{:T(128)S(6)} %div.38), kind=kOutput, calls=%fused_computation.42 | convolution fusion | flops 12889096192 | bytes 12582916 | tf_op jit(solution)/shard_map/dot_general | solution.py:72
  288.4 2.5 fusion.15
  290.9 2.5 convolution_divide_fusion.1
  293.4 2.5 convolution_divide_fusion
  297.2 101.8 %all_to_all.5 = bf16[32,32,2048]{2,1,0:T(8,128)(2,1)S(1)} all-to-all(bf16[32,32,2048]{2,1,0:T(8,128)(2,1)S(1)} %stack.2), channel_id=1, replica_groups=mesh['row'=32,'col'=8] {'row'}, dimensions={0} | all-to-all | bytes 8388608 | tf_op jit(solution)/shard_map/all_to_all | solution.py:85
  401.5 1.3 copy-done.3
  402.8 1.7 multiply_reduce_fusion
  404.5 75.9 %all-reduce = (f32[]{:T(128)}, f32[]{:T(128)}) all-reduce(f32[]{:T(128)} %get-tuple-element.17, f32[]{:T(128)} %multiply_reduce_fusion), channel_id=1, replica_groups=mesh['row'=32,'col'=8] {'row','col'}, use_global_device_ids=true, to_apply=%region_4.5 | all-reduce | flops 2 | bytes 16 | tf_op jit(solution)/shard_map/psum | solution.py:95
  481.7 3.4 multiply_convert_fusion
  (25 shorter events, 8.1 us)
Async XLA Ops:
  7.2 1.2 copy-start
  7.2 162.9 %reduce-scatter.4.cloned.1.call-start = ((), (), s32[]{:S(2)}) async-start(), calls=%async_computation.3 | async-start | bytes 8650752
  14.1 7.2 %collective-permute-start = (bf16[512,2048]{1,0:T(8,128)(2,1)S(1)}, bf16[512,2048]{1,0:T(8,128)(2,1)}, u32[]{:S(2)}, u32[]{:S(2)}) collective-permute-start(bf16[512,2048]{1,0:T(8,128)(2,1)S(1)} %get-tuple-element.18), channel_id=1, source_target_pairs={{0,8},{8,0},{16,24},{24,16},{32,40},{40,32},{48,56},{56,48},{64,72... | collective-permute-start | bytes 6291464 | tf_op jit(solution)/shard_map/ppermute | solution.py:18
  26.2 2.6 copy-start.5
  42.0 0.9 copy-start.4
  42.1 205.1 %all-gather.2.cloned.1.call-start = ((), (), s32[]{:S(2)}) async-start(), calls=%async_computation.2 | async-start | bytes 8650752 | tf_op jit(solution)/shard_map/all_gather | solution.py:52
  252.7 5.8 %copy-start.2 = (f32[1024,2048]{1,0:T(8,128)S(1)}, f32[1024,2048]{1,0:T(8,128)}, u32[]{:S(2)}) copy-start(f32[1024,2048]{1,0:T(8,128)} %all-gather.2.cloned.1.call-done) | copy-start | bytes 25165828
  297.2 101.8 %copy-start.6 = (bf16[512,2048]{0,1:T(8,128)(2,1)S(1)}, bf16[512,2048]{0,1:T(8,128)(2,1)}, u32[]{:S(2)}) copy-start(bf16[512,2048]{0,1:T(8,128)(2,1)} %copy-done.5) | copy-start | bytes 6291460
  401.5 1.3 copy-start.3
  402.8 82.3 %copy-start.1 = (bf16[1024,512]{1,0:T(8,128)(2,1)S(1)}, bf16[1024,512]{1,0:T(8,128)(2,1)}, u32[]{:S(2)}) copy-start(bf16[1024,512]{1,0:T(8,128)(2,1)} %param.5) | copy-start | bytes 3145732
Sparse Core Ops, SparseCore 0:
  42.2 127.8 reduce-scatter.3
  172.7 74.4 all-gather.1
